TPU v7x, 32 devices: a whole 2x2x4 slice. The times are simulated.
32 devices in a mesh: pheno: 2 (over x), samp: 8 (over z, y), var: 2 (over core).
Axes of the slice: x: 2, y: 2, z: 4, core: 2. Of those that a mesh axis runs over, the one named last changes fastest.
Arguments:
- genotypes: bfloat16 [4608, 16384], P('samp', 'var'), may hold values from -6 to 6, as said below
- coefficients: float32 [64, 16384], P('pheno', 'var'), parts along dimension 0, may hold values from -0.5 to 0.5
- time_order: int32 [9216], P(('pheno', 'samp')), parts along dimension 0, may hold values from 0 to 4607, as said below
- fold_label: int32 [9216], P(('pheno', 'samp')), parts along dimension 0, may hold values from 0 to 7
- event_flag: int32 [9216], P(('pheno', 'samp')), parts along dimension 0, may hold values 0 or 1
- penalty: float32 [32], replicated, may hold values from 0.3 to 1.5
- step_size: float32 [32], replicated, may hold values from 0.2 to 1
Outputs:
- coefficients_out: float32 [64, 16384], P('pheno', 'var'), parts along dimension 0
- score: bfloat16 [64, 4608], P('pheno', 'samp'), parts along dimension 0
There are 2 independent parts, one for each index of `pheno`. A program takes and returns all parts, laid end to end along the dimension named above; an argument that names none is the same for every part. Nothing has to cross between parts.
Inputs may be any that keep to these rules, and one draw needn't show every extreme that they name: time_order names every sample ID once; each block of 576 consecutive IDs holds exactly 576 / 8 of the IDs in each block of 576 consecutive time ranks. `genotypes`: entries of mean zero and unit variance.
All inputs are finite; a program needn't handle non-finite values. No bound on the sum of `event_flag` on one device may be relied on, other than what follows from the above.
Results may differ from a plain program's by a relative error of at most 0.0027.
Values may be sent and summed in bfloat16 or wider, within the bound.
A program may use at most 64 MiB of HBM per device.

v0:
```python
import math

import jax
import jax.numpy as jnp
from jax import lax
from jax.sharding import PartitionSpec as P

VARS = 16384
FOLDS = 8
ITERS = 3


def carried_in(value, axis, join, neutral, backward):
    count, mine = (lax.axis_size(axis), lax.axis_index(axis))
    pieces = lax.all_gather(value, axis)
    if backward:
        pieces = pieces[::-1]
        mine = count - 1 - mine
    subtotal = jnp.full_like(value, 0) + jnp.asarray(neutral, value.dtype)

    def lap(position, subtotal):
        longer = join(subtotal, pieces[position])
        return jnp.where(position < mine, longer, subtotal)

    return lax.fori_loop(0, count - 1, lap, subtotal)


def shrink(coef, gradient, penalty, step_size):
    stepped = coef - step_size[:, None] * gradient
    threshold = (step_size * penalty)[:, None]
    return jnp.sign(stepped) * jnp.maximum(jnp.abs(stepped) - threshold, 0.0)


def local(genotypes, coefficients, time_order, fold_label, event_flag, penalty, step_size):
    block_rows = genotypes.shape[0]
    columns = coefficients.shape[0]
    position = lax.axis_index("samp")
    order_all, fold_all, event_all = (
        lax.all_gather(time_order, "samp", axis=0, tiled=True),
        lax.all_gather(fold_label, "samp", axis=0, tiled=True),
        lax.all_gather(event_flag, "samp", axis=0, tiled=True),
    )
    sample_count = order_all.shape[0]
    first_rank = position * block_rows
    ids_time = lax.dynamic_slice_in_dim(order_all, first_rank, block_rows)
    inverse = (
        jnp.zeros((sample_count,), jnp.int32)
        .at[order_all]
        .set(jnp.arange(sample_count, dtype=jnp.int32))
    )
    rank_mine = lax.dynamic_slice_in_dim(inverse, position * block_rows, block_rows)
    owner_mine = rank_mine // block_rows
    send_order = jnp.argsort(owner_mine, stable=True)
    send_back = jnp.argsort(send_order, stable=True)
    sorted_ids = jnp.argsort(ids_time, stable=True)
    slot_of_rank = jnp.argsort(sorted_ids, stable=True)
    column_fold = jnp.arange(columns, dtype=jnp.int32) % FOLDS
    fold_time = fold_all[ids_time]
    event_time = event_all[ids_time].astype(jnp.float32)
    train_mask = (fold_time[None, :] != column_fold[:, None]).astype(jnp.float32)
    events_kept = train_mask * event_time[None, :]
    zero_column = jnp.zeros((columns,), jnp.float32)
    scale_vars = 1.0 / math.sqrt(VARS)
    scale_samples = 1.0 / math.sqrt(sample_count)
    coef = coefficients
    score_mine = jnp.zeros((columns, block_rows), jnp.bfloat16)
    for step in range(ITERS):
        coef_low = coef.astype(jnp.bfloat16)
        partial_value = lax.dot_general(
            coef_low, genotypes, (((1,), (1,)), ((), ())), preferred_element_type=jnp.float32
        )
        predictor = lax.psum(partial_value, "var") * scale_vars
        outgoing = predictor[:, send_order]
        arrived = lax.all_to_all(outgoing, "samp", split_axis=1, concat_axis=1, tiled=True)
        predictor_time = arrived[:, slot_of_rank]
        weight = train_mask * jnp.exp(predictor_time)
        local_risk = lax.cumsum(weight, axis=1, reverse=True)
        block_weight = local_risk[:, 0]
        later_risk = carried_in(block_weight, "samp", jnp.add, zero_column, True)
        risk = local_risk + later_risk[:, None]
        ratio = events_kept / jnp.where(events_kept > 0, risk, 1.0)
        local_hazard = lax.cumsum(ratio, axis=1)
        block_ratio = local_hazard[:, -1]
        earlier_sum = carried_in(block_ratio, "samp", jnp.add, zero_column, False)
        hazard = local_hazard + earlier_sum[:, None]
        score_time = (weight * hazard - events_kept).astype(jnp.bfloat16)
        returning = score_time[:, sorted_ids]
        came_back = lax.all_to_all(returning, "samp", split_axis=1, concat_axis=1, tiled=True)
        score_mine = came_back[:, send_back]
        grad_partial = jnp.dot(score_mine, genotypes, preferred_element_type=jnp.float32)
        gradient = lax.psum(grad_partial, "samp") * scale_samples
        coef = shrink(coef, gradient, penalty, step_size)
    return (coef, score_mine)


def solution(mesh):
    placed = (
        P("samp", "var"),
        P("pheno", "var"),
        P(("pheno", "samp")),
        P(("pheno", "samp")),
        P(("pheno", "samp")),
        P(),
        P(),
    )
    return jax.shard_map(
        local,
        mesh=mesh,
        in_specs=placed,
        out_specs=(P("pheno", "var"), P("pheno", "samp")),
        check_vma=False,
    )
```

profile of v0, /device:TPU:24, one launch (start us, length us, event | category | flops | bytes accessed | tf_op | source)
XLA Modules:
  0.0 636.4 jit_solution(7158025991990712749)
XLA Ops:
  7.3 7.5 %fusion.4 = f32[32,576]{1,0:T(8,128)} fusion(bf16[576,8192]{1,0:T(8,128)(2,1)} %param.19, f32[32,8192]{1,0:T(8,128)} %param.20), kind=kOutput, calls=%fused_computation.44 | convolution fusion | flops 302252032 | bytes 10559488 | tf_op jit(solution)/shard_map/dot_general | solution.py:69
  16.8 34.9 %all-reduce.15 = (s32[4608]{0:T(1024)S(1)}, s32[4608]{0:T(1024)S(1)}, s32[4608]{0:T(1024)S(1)}) all-reduce(s32[4608]{0:T(1024)S(1)} %dynamic-update-slice.1, s32[4608]{0:T(1024)S(1)} %dynamic-update-slice, s32[4608]{0:T(1024)S(1)} %dynamic-update-slice.2), channel_id=1, replica_groups=mesh['pheno'=2,'samp'=8,'var'=2] {'samp'}, use_global_device_ids=true, to_apply=%add.7 | all-reduce | flops 13824 | bytes 110592
  51.7 17.4 %scatter_custom_fusion = s32[4608]{0:T(1024)S(1)} fusion(s32[4608]{0:T(1024)S(1)} %compare_select_fusion.3, s32[4608]{0:T(1024)S(1)} %iota.22, s32[]{:T(128)} %copy.192), kind=kCustom, calls=%fused_computation.82 | custom fusion | bytes 18436 | tf_op jit(solution)/shard_map/scatter | solution.py:49
  69.2 4.4 sort.60
  73.6 4.4 sort.61
  78.0 4.4 sort.59
  82.4 4.4 sort.62
  90.2 6.6 %all-to-all-start = ((f32[32,8,72]{2,0,1:T(8,128)}), f32[32,8,72]{2,0,1:T(8,128)S(1)}, u32[]{:S(2)}, u32[]{:S(2)}) async-start(f32[32,8,72]{2,0,1:T(8,128)} %copy.64), calls=%async_computation | async-start | bytes 262144 | tf_op jit(solution)/shard_map/all_to_all | solution.py:74
  106.6 6.2 reduce-window.40
  113.5 16.8 %all-reduce.9 = f32[256]{0:T(256)S(1)} all-reduce(f32[256]{0:T(256)S(1)} %dynamic-update-slice.3), channel_id=2, replica_groups=mesh['pheno'=2,'samp'=8,'var'=2] {'samp'}, use_global_device_ids=true, to_apply=%add.9 | all-reduce | flops 256 | bytes 2048
  133.4 18.6 %all-reduce.10 = f32[256]{0:T(256)S(1)} all-reduce(f32[256]{0:T(256)S(1)} %dynamic-update-slice.4), channel_id=3, replica_groups=mesh['pheno'=2,'samp'=8,'var'=2] {'samp'}, use_global_device_ids=true, to_apply=%add.10 | all-reduce | flops 256 | bytes 2048
  155.4 6.8 %all-to-all-start.1 = ((bf16[32,8,72]{2,0,1:T(8,128)(2,1)}), bf16[32,8,72]{2,0,1:T(8,128)(2,1)S(1)}, u32[]{:S(2)}, u32[]{:S(2)}) async-start(bf16[32,8,72]{2,0,1:T(8,128)(2,1)} %copy.72), calls=%async_computation.1 | async-start | bytes 131072 | tf_op jit(solution)/shard_map/all_to_all | solution.py:88
  167.9 6.4 %fusion.12 = f32[32,8192]{1,0:T(8,128)} fusion(bf16[576,32]{1,0:T(8,128)(2,1)S(1)} %gather_fusion.5, bf16[576,8192]{1,0:T(8,128)(2,1)} %param.19), kind=kOutput, calls=%fused_computation.95 | convolution fusion | flops 301989888 | bytes 10522624 | tf_op jit(solution)/shard_map/dot_general | solution.py:90
  174.5 77.5 %all-reduce.25.cloned.1.call-done = f32[32,8192]{1,0:T(8,128)} async-done(((f32[32,8192]{1,0:T(8,128)}), f32[32,8192]{1,0:T(8,128)}) %all-reduce.25.cloned.1.call-update) | async-done | bytes 1048592 | tf_op jit(solution)/shard_map/psum | solution.py:91
  252.0 7.5 %fusion.2 = f32[32,576]{1,0:T(8,128)} fusion(bf16[576,8192]{1,0:T(8,128)(2,1)} %param.19, f32[32,8192]{1,0:T(8,128)S(1)} %copy-done, f32[32,8192]{1,0:T(8,128)} %all-reduce.25.cloned.1.call-done, f32[32]{0:T(128)S(1)} %get-tuple-element.642, f32[32]{0:T(128)S(1)} %get-tuple-element.641), kind=kOutput, calls=%fused_computation.42 | convolution fusion | flops 304087040 | bytes 11608320 | tf_op jit(solution)/shard_map/dot_general | solution.py:69
  259.4 19.0 %all-reduce.27.cloned.1.call-done = f32[32,576]{1,0:T(8,128)} async-done(((f32[32,576]{1,0:T(8,128)}), f32[32,576]{1,0:T(8,128)}) %all-reduce.27.cloned.1.call-update) | async-done | bytes 73744 | tf_op jit(solution)/shard_map/psum | solution.py:72
  281.9 6.0 all-to-all-start.2
  294.2 6.2 reduce-window.46
  301.0 16.9 %all-reduce.11 = f32[256]{0:T(256)S(1)} all-reduce(f32[256]{0:T(256)S(1)} %dynamic-update-slice.5), channel_id=4, replica_groups=mesh['pheno'=2,'samp'=8,'var'=2] {'samp'}, use_global_device_ids=true, to_apply=%add.11 | all-reduce | flops 256 | bytes 2048
  320.9 18.5 %all-reduce.12 = f32[256]{0:T(256)S(1)} all-reduce(f32[256]{0:T(256)S(1)} %dynamic-update-slice.6), channel_id=5, replica_groups=mesh['pheno'=2,'samp'=8,'var'=2] {'samp'}, use_global_device_ids=true, to_apply=%add.12 | all-reduce | flops 256 | bytes 2048
  342.2 10.3 %all_to_all.72 = bf16[32,8,72]{2,0,1:T(8,128)(2,1)S(1)} all-to-all(bf16[32,8,72]{2,0,1:T(8,128)(2,1)S(1)} %copy.83), channel_id=1, replica_groups=mesh['pheno'=2,'samp'=8,'var'=2] {'samp'}, dimensions={1} | all-to-all | bytes 73728 | tf_op jit(solution)/shard_map/all_to_all | solution.py:88
  354.6 6.4 %fusion.13 = f32[32,8192]{1,0:T(8,128)} fusion(bf16[576,32]{1,0:T(8,128)(2,1)S(1)} %gather_fusion.9, bf16[576,8192]{1,0:T(8,128)(2,1)} %param.19), kind=kOutput, calls=%fused_computation.96 | convolution fusion | flops 301989888 | bytes 10522624 | tf_op jit(solution)/shard_map/dot_general | solution.py:90
  361.3 77.1 %all-reduce.29.cloned.1.call-done = f32[32,8192]{1,0:T(8,128)} async-done(((f32[32,8192]{1,0:T(8,128)}), f32[32,8192]{1,0:T(8,128)}) %all-reduce.29.cloned.1.call-update) | async-done | bytes 1048592 | tf_op jit(solution)/shard_map/psum | solution.py:91
  440.6 7.2 %fusion = f32[32,576]{1,0:T(8,128)} fusion(bf16[576,8192]{1,0:T(8,128)(2,1)} %param.19, f32[32,8192]{1,0:T(8,128)S(1)} %maximum_multiply_fusion.1), kind=kOutput, calls=%fused_computation.40 | convolution fusion | flops 302252032 | bytes 10559488 | tf_op jit(solution)/shard_map/dot_general | solution.py:69
  447.8 19.0 %all-reduce.31.cloned.1.call-done = f32[32,576]{1,0:T(8,128)} async-done(((f32[32,576]{1,0:T(8,128)}), f32[32,576]{1,0:T(8,128)}) %all-reduce.31.cloned.1.call-update) | async-done | bytes 73744 | tf_op jit(solution)/shard_map/psum | solution.py:72
  470.3 6.0 all-to-all-start.4
  482.5 6.2 reduce-window.54
  489.3 16.9 %all-reduce.13 = f32[256]{0:T(256)S(1)} all-reduce(f32[256]{0:T(256)S(1)} %dynamic-update-slice.7), channel_id=6, replica_groups=mesh['pheno'=2,'samp'=8,'var'=2] {'samp'}, use_global_device_ids=true, to_apply=%add.13 | all-reduce | flops 256 | bytes 2048
  509.3 18.5 %all-reduce.14 = f32[256]{0:T(256)S(1)} all-reduce(f32[256]{0:T(256)S(1)} %dynamic-update-slice.8), channel_id=7, replica_groups=mesh['pheno'=2,'samp'=8,'var'=2] {'samp'}, use_global_device_ids=true, to_apply=%add.14 | all-reduce | flops 256 | bytes 2048
  530.6 10.3 %all_to_all.73 = bf16[32,8,72]{2,0,1:T(8,128)(2,1)S(1)} all-to-all(bf16[32,8,72]{2,0,1:T(8,128)(2,1)S(1)} %copy.94), channel_id=1, replica_groups=mesh['pheno'=2,'samp'=8,'var'=2] {'samp'}, dimensions={1} | all-to-all | bytes 73728 | tf_op jit(solution)/shard_map/all_to_all | solution.py:88
  542.9 6.4 %fusion.14 = f32[32,8192]{1,0:T(8,128)} fusion(bf16[576,32]{1,0:T(8,128)(2,1)S(1)} %gather_fusion.13, bf16[576,8192]{1,0:T(8,128)(2,1)} %param.19), kind=kOutput, calls=%fused_computation.97 | convolution fusion | flops 301989888 | bytes 10522624 | tf_op jit(solution)/shard_map/dot_general | solution.py:90
  550.1 76.7 %all-reduce.33.cloned.1.call-done = f32[32,8192]{1,0:T(8,128)} async-done(((f32[32,8192]{1,0:T(8,128)}), f32[32,8192]{1,0:T(8,128)}) %all-reduce.33.cloned.1.call-update) | async-done | bytes 1048592 | tf_op jit(solution)/shard_map/psum | solution.py:91
  (226 shorter events, 69.8 us)
Async XLA Ops:
  7.2 7.6 %copy-start.7 = (u32[32]{0:T(128)S(1)}, u32[32]{0:T(128)}, u32[]{:S(2)}) copy-start(u32[32]{0:T(128)} %constant.209) | copy-start | bytes 388
  7.2 8.7 %copy-start.2 = (s32[576]{0:T(1024)S(1)}, s32[576]{0:T(1024)}, u32[]{:S(2)}) copy-start(s32[576]{0:T(1024)} %param.22) | copy-start | bytes 6916
  7.2 9.0 %copy-start.3 = (s32[576]{0:T(1024)S(1)}, s32[576]{0:T(1024)}, u32[]{:S(2)}) copy-start(s32[576]{0:T(1024)} %param.21) | copy-start | bytes 6916
  7.2 9.3 %copy-start.4 = (s32[576]{0:T(1024)S(1)}, s32[576]{0:T(1024)}, u32[]{:S(2)}) copy-start(s32[576]{0:T(1024)} %param.23) | copy-start | bytes 6916
  7.2 79.6 %all-reduce.23.cloned.1.call-start = ((), (), s32[]{:S(2)}) async-start(), calls=%async_computation.6 | async-start | bytes 163840 | tf_op jit(solution)/shard_map/psum | solution.py:72
  90.2 14.3 %all-to-all-start = ((f32[32,8,72]{2,0,1:T(8,128)}), f32[32,8,72]{2,0,1:T(8,128)S(1)}, u32[]{:S(2)}, u32[]{:S(2)}) async-start(f32[32,8,72]{2,0,1:T(8,128)} %copy.64), calls=%async_computation | async-start | bytes 262144 | tf_op jit(solution)/shard_map/all_to_all | solution.py:74
  131.0 43.4 %copy-start.5 = (f32[32]{0:T(128)S(1)}, f32[32]{0:T(128)}, u32[]{:S(2)}) copy-start(f32[32]{0:T(128)} %param.25) | copy-start | bytes 388
  131.0 43.4 %copy-start.6 = (f32[32]{0:T(128)S(1)}, f32[32]{0:T(128)}, u32[]{:S(2)}) copy-start(f32[32]{0:T(128)} %param.24) | copy-start | bytes 388
  131.0 120.9 %copy-start = (f32[32,8192]{1,0:T(8,128)S(1)}, f32[32,8192]{1,0:T(8,128)}, u32[]{:S(2)}) copy-start(f32[32,8192]{1,0:T(8,128)} %param.20) | copy-start | bytes 3145732
  155.4 10.5 %all-to-all-start.1 = ((bf16[32,8,72]{2,0,1:T(8,128)(2,1)}), bf16[32,8,72]{2,0,1:T(8,128)(2,1)S(1)}, u32[]{:S(2)}, u32[]{:S(2)}) async-start(bf16[32,8,72]{2,0,1:T(8,128)(2,1)} %copy.72), calls=%async_computation.1 | async-start | bytes 131072 | tf_op jit(solution)/shard_map/all_to_all | solution.py:88
  162.2 89.7 %all-reduce.25.cloned.1.call-start = ((), (), s32[]{:S(2)}) async-start(), calls=%async_computation.7 | async-start | bytes 2097152 | tf_op jit(solution)/shard_map/psum | solution.py:91
  174.4 104.1 %all-reduce.27.cloned.1.call-start = ((), (), s32[]{:S(2)}) async-start(), calls=%async_computation.8 | async-start | bytes 163840 | tf_op jit(solution)/shard_map/psum | solution.py:72
  281.9 10.1 %all-to-all-start.2 = ((f32[32,8,72]{2,0,1:T(8,128)}), f32[32,8,72]{2,0,1:T(8,128)S(1)}, u32[]{:S(2)}, u32[]{:S(2)}) async-start(f32[32,8,72]{2,0,1:T(8,128)} %copy.75), calls=%async_computation.2 | async-start | bytes 262144 | tf_op jit(solution)/shard_map/all_to_all | solution.py:74
  287.9 150.5 %all-reduce.29.cloned.1.call-start = ((), (), s32[]{:S(2)}) async-start(), calls=%async_computation.9 | async-start | bytes 2097152 | tf_op jit(solution)/shard_map/psum | solution.py:91
  318.6 119.8 %copy-start.1 = (f32[32,8192]{1,0:T(8,128)S(1)}, f32[32,8192]{1,0:T(8,128)}, u32[]{:S(2)}) copy-start(f32[32,8192]{1,0:T(8,128)} %all-reduce.25.cloned.1.call-done) | copy-start | bytes 3145732
  361.0 105.8 %all-reduce.31.cloned.1.call-start = ((), (), s32[]{:S(2)}) async-start(), calls=%async_computation.10 | async-start | bytes 163840 | tf_op jit(solution)/shard_map/psum | solution.py:72
  470.3 10.1 %all-to-all-start.4 = ((f32[32,8,72]{2,0,1:T(8,128)}), f32[32,8,72]{2,0,1:T(8,128)S(1)}, u32[]{:S(2)}, u32[]{:S(2)}) async-start(f32[32,8,72]{2,0,1:T(8,128)} %copy.86), calls=%async_computation.4 | async-start | bytes 262144 | tf_op jit(solution)/shard_map/all_to_all | solution.py:74
  476.3 150.5 %all-reduce.33.cloned.1.call-start = ((), (), s32[]{:S(2)}) async-start(), calls=%async_computation.11 | async-start | bytes 2097152 | tf_op jit(solution)/shard_map/psum | solution.py:91
Sparse Core Ops, SparseCore 0:
  14.9 19.0 all-reduce.22
  174.5 77.4 all-reduce.24
  259.6 18.8 all-reduce.26
  361.1 77.2 all-reduce.28
  447.9 18.8 all-reduce.30
  549.5 77.2 all-reduce.32
where the time goes:
time: 640 us; the launch traced here: 636 us
  waiting for transfers between devices  281 us (44%)
  blocking collectives  162 us (25%)
  local copies, waits for them, and re-layouts  58.1 us (9%)
  other arithmetic  51.5 us (8%)
  matrix products  41.3 us (6%)
  starting transfers between devices  25.8 us (4%)
  between operations  15.9 us (2%)
    psum x3, waiting for transfers between devices, local(): gradient = lax.psum(grad_partial, 'samp') * scale_samples  231 us
    unnamed x7, blocking collectives  141 us
    psum x3, waiting for transfers between devices, local(): predictor = lax.psum(partial_value, 'var') * scale_vars  38.1 us
    another operation x12, other arithmetic  23.2 us
    dot_general x3, matrix products, local(): lax.dot_general(coef_low, genotypes, (((1,), (1,)), ((), ())), preferred_...  22.1 us
    all_to_all x2, blocking collectives, local(): lax.all_to_all(returning, 'samp', split_axis=1, concat_axis=1, tiled=True)  20.5 us
    dot_general x3, matrix products, local(): jnp.dot(score_mine, genotypes, preferred_element_type=jnp.float32)  19.2 us
    all_to_all x3, starting transfers between devices, local(): lax.all_to_all(outgoing, 'samp', split_axis=1, concat_axis=1, tiled=True)  18.6 us
  transfers between devices with their start and end apart: 10, of which 8 were waited for; matrix products, arithmetic and copies ran while one was open for 7% of the time, Pallas kernels for 0%

commit v1 on v0

v1 whole, which is shorter than its diff:
```python
import functools
import math

import jax
import jax.numpy as jnp
from jax import lax
from jax.experimental import pallas as pl
from jax.experimental.pallas import tpu as pltpu
from jax.sharding import PartitionSpec as P

VARS = 16384
FOLDS = 8
ITERS = 3
MESH = pl.DeviceIdType.MESH
F32 = jnp.float32
BF16 = jnp.bfloat16


def each(count, body):
    if count <= 8:
        for step in range(count):
            body(step)
    else:
        lax.fori_loop(0, count, lambda step, carry: (body(step), carry)[1], 0)


def halves(value):
    high = value.astype(BF16)
    low = (value - high.astype(F32)).astype(BF16)
    return jnp.concatenate([high, low], axis=0)


def dot2(value, matrix):
    rows = value.shape[0]
    both = jnp.dot(halves(value), matrix, preferred_element_type=F32)
    return both[:rows] + both[rows:]


def path_kernel(
    count, scale_vars, scale_samples,
    geno, coef_in, to_time, later, earlier, to_id, mask, kept, kept_time, step_size, penalty,
    coef_out, score_out,
    low, shard, half_send, half_recv, out_a, in_a, out_b, in_b, out_g, in_g, pred,
    half_ss, half_rs, a_ss, a_rs, b_ss, b_rs, g_ss, g_rs, c_ss, c_rs, f_ss, f_rs,
):
    me = lax.axis_index("samp")
    var = lax.axis_index("var")
    columns, variants = coef_in.shape
    rows = geno.shape[0]
    part = variants // count
    width = later.shape[0] // count

    def peer(step):
        return lax.rem(me + step, count)

    def piece(owner):
        return pl.ds(pl.multiple_of(owner * part, part), part)

    def slots(owner):
        return pl.ds(pl.multiple_of(owner * width, width), width)

    barrier = pltpu.get_barrier_semaphore()

    def greet(step):
        pl.semaphore_signal(barrier, inc=1, device_id={"samp": peer(step + 1)}, device_id_type=MESH)

    each(count - 1, greet)
    pl.semaphore_signal(barrier, inc=1, device_id={"var": 1 - var}, device_id_type=MESH)
    pl.semaphore_wait(barrier, count)

    def send(source, target, ssem, rsem, owner):
        return pltpu.make_async_remote_copy(
            src_ref=source,
            dst_ref=target,
            send_sem=ssem.at[owner],
            recv_sem=rsem.at[me],
            device_id={"samp": owner},
            device_id_type=MESH,
        )

    def arrive(source, target, ssem, rsem, owner):
        pltpu.make_async_remote_copy(
            src_ref=source,
            dst_ref=target,
            send_sem=ssem.at[owner],
            recv_sem=rsem.at[owner],
            device_id={"samp": owner},
            device_id_type=MESH,
        ).wait_recv()

    def fill(step):
        low[step] = coef_in[:, piece(step)].astype(BF16)

    each(count, fill)
    shard[...] = coef_in[:, piece(me)]

    def one_step(turn, carry):
        pred[...] = jnp.zeros_like(pred)

        def add_part(step):
            owner = peer(step)
            if not (isinstance(step, int) and step == 0):
                @pl.when(turn > 0)
                def _():
                    if isinstance(step, int):
                        arrive(low.at[owner], low.at[owner], c_ss, c_rs, owner)
                    else:
                        @pl.when(step > 0)
                        def _():
                            arrive(low.at[owner], low.at[owner], c_ss, c_rs, owner)
            pred[...] += lax.dot_general(
                low[owner], geno[:, piece(owner)], (((1,), (1,)), ((), ())), preferred_element_type=F32
            )

        each(count, add_part)
        half_send[...] = pred[...]
        slot = lax.rem(turn, 2)
        swap = pltpu.make_async_remote_copy(
            src_ref=half_send, dst_ref=half_recv.at[slot], send_sem=half_ss, recv_sem=half_rs.at[slot],
            device_id={"var": 1 - var}, device_id_type=MESH,
        )
        swap.start()
        swap.wait()

        @pl.when(turn > 0)
        def _():
            def drained(step):
                owner = peer(step + 1)
                send(low.at[me], low.at[me], c_ss, c_rs, owner).wait_send()
            each(count - 1, drained)

        weight = mask[...] * jnp.exp((half_send[...] + half_recv[slot]) * scale_vars)
        pred[...] = weight
        spread = dot2(weight, to_time[...])
        for owner in range(count):
            out_a[owner] = spread[:, owner * width:(owner + 1) * width]

        def push_a(step):
            owner = peer(step + 1)
            send(out_a.at[owner], in_a.at[me], a_ss, a_rs, owner).start()
        each(count - 1, push_a)
        risk = dot2(out_a[me], later[slots(me), :])
        for step in range(count - 1):
            owner = peer(step + 1)
            arrive(out_a.at[owner], in_a.at[owner], a_ss, a_rs, owner)
            risk += dot2(in_a[owner], later[slots(owner), :])
        events = kept_time[...]
        ratio = events / jnp.where(events > 0, risk, 1.0)
        spread = dot2(ratio, earlier[...])
        for owner in range(count):
            out_b[owner] = spread[:, owner * width:(owner + 1) * width]

        def push_b(step):
            owner = peer(step + 1)
            send(out_b.at[owner], in_b.at[me], b_ss, b_rs, owner).start()
        each(count - 1, push_b)
        hazard = dot2(out_b[me], to_id[slots(me), :])
        for step in range(count - 1):
            owner = peer(step + 1)
            arrive(out_b.at[owner], in_b.at[owner], b_ss, b_rs, owner)
            hazard += dot2(in_b[owner], to_id[slots(owner), :])
        score_out[...] = (pred[...] * hazard - kept[...]).astype(BF16)

        def push_g(step):
            owner = peer(step + 1)
            out_g[owner] = jnp.dot(
                score_out[...], geno[:, piece(owner)], preferred_element_type=F32
            ).astype(out_g.dtype)
            send(out_g.at[owner], in_g.at[me], g_ss, g_rs, owner).start()
        each(count - 1, push_g)
        total = jnp.dot(score_out[...], geno[:, piece(me)], preferred_element_type=F32)
        for step in range(count - 1):
            owner = peer(count - 1 - step)
            arrive(out_g.at[owner], in_g.at[owner], g_ss, g_rs, owner)
            total += in_g[owner].astype(F32)
        pace = step_size[...]
        stepped = shard[...] - pace * (total * scale_samples)
        shrunk = jnp.maximum(jnp.abs(stepped) - pace * penalty[...], 0.0)
        fresh = jnp.where(stepped > 0, shrunk, -shrunk)
        shard[...] = fresh

        def drained_all(step):
            owner = peer(step + 1)
            send(out_a.at[owner], in_a.at[me], a_ss, a_rs, owner).wait_send()
            send(out_b.at[owner], in_b.at[me], b_ss, b_rs, owner).wait_send()
            send(out_g.at[owner], in_g.at[me], g_ss, g_rs, owner).wait_send()

        @pl.when(turn < ITERS - 1)
        def _():
            low[me] = fresh.astype(BF16)

            def push_c(step):
                owner = peer(step + 1)
                send(low.at[me], low.at[me], c_ss, c_rs, owner).start()
            each(count - 1, push_c)

        each(count - 1, drained_all)
        return carry

    lax.fori_loop(0, ITERS, one_step, 0)

    coef_out[:, piece(me)] = shard[...]

    def push_f(step):
        owner = peer(step + 1)
        send(shard, coef_out.at[:, piece(me)], f_ss, f_rs, owner).start()
    each(count - 1, push_f)

    def land_f(step):
        owner = peer(step + 1)
        arrive(shard, coef_out.at[:, piece(owner)], f_ss, f_rs, owner)
        send(shard, coef_out.at[:, piece(me)], f_ss, f_rs, owner).wait_send()
    each(count - 1, land_f)


def local(genotypes, coefficients, time_order, fold_label, event_flag, penalty, step_size):
    rows = genotypes.shape[0]
    columns, variants = coefficients.shape
    count = lax.axis_size("samp")
    me = lax.axis_index("samp")
    share = rows // count
    width = -(-(share + count) // 128) * 128
    total = count * width
    part = variants // count

    ranks = jnp.arange(rows, dtype=jnp.int32)
    slot_all = jnp.arange(total, dtype=jnp.int32)
    lane = slot_all % width
    group = slot_all // width
    owner = time_order // rows
    place = time_order % rows
    same = (owner[:, None] == owner[None, :]) & (ranks[:, None] < ranks[None, :])
    key = owner * width + jnp.sum(same.astype(jnp.int32), axis=0)
    match = key[:, None] == slot_all[None, :]
    rank_of = jnp.max(jnp.where(match, ranks[:, None], -1), axis=0)
    place_of = jnp.max(jnp.where(match, place[:, None], -1), axis=0)
    place_in = lax.all_to_all(place_of.reshape(count, width), "samp", 0, 0, tiled=True).reshape(total)
    match_id = place_in[None, :] == ranks[:, None]
    code = fold_label * 2 + event_flag
    code_out = jnp.sum(jnp.where(match_id, code[:, None], 0), axis=0)
    code_in = lax.all_to_all(code_out.reshape(count, width), "samp", 0, 0, tiled=True).reshape(total)
    code_time = jnp.sum(jnp.where(rank_of[None, :] == ranks[:, None], code_in[None, :], 0), axis=1)
    block = jnp.sum(jnp.where(match_id, group[None, :], 0), axis=1)

    in_totals = (lane >= share) & (lane < share + count)
    to_time = (match_id | (in_totals[None, :] & ((lane - share)[None, :] == block[:, None]))).astype(BF16)
    reach = jnp.where(lane < share, rank_of, jnp.where(in_totals & (lane - share > me), rows, -1))
    later = (reach[:, None] >= ranks[None, :]).astype(BF16)
    back = jnp.where(lane < share, rank_of, jnp.where(lane == share, rows, -1))
    earlier = (ranks[:, None] <= back[None, :]).astype(BF16)
    to_id = (
        (place_in[:, None] == ranks[None, :])
        | ((lane == share)[:, None] & (group[:, None] < block[None, :]))
    ).astype(BF16)

    column_fold = jnp.arange(columns, dtype=jnp.int32) % FOLDS
    mask = (fold_label[None, :] != column_fold[:, None]).astype(F32)
    kept = mask * event_flag.astype(F32)[None, :]
    kept_time = ((code_time // 2)[None, :] != column_fold[:, None]).astype(F32) * (code_time % 2).astype(F32)[None, :]

    vmem = pl.BlockSpec(memory_space=pltpu.VMEM)
    dma = pltpu.SemaphoreType.DMA
    return pl.pallas_call(
        functools.partial(path_kernel, count, 1.0 / math.sqrt(VARS), 1.0 / math.sqrt(rows * count)),
        out_shape=(
            jax.ShapeDtypeStruct((columns, variants), F32),
            jax.ShapeDtypeStruct((columns, rows), BF16),
        ),
        in_specs=[vmem] * 11,
        out_specs=(vmem, vmem),
        scratch_shapes=[
            pltpu.VMEM((count, columns, part), BF16),
            pltpu.VMEM((columns, part), F32),
            pltpu.VMEM((columns, rows), F32),
            pltpu.VMEM((2, columns, rows), F32),
            pltpu.VMEM((count, columns, width), F32),
            pltpu.VMEM((count, columns, width), F32),
            pltpu.VMEM((count, columns, width), F32),
            pltpu.VMEM((count, columns, width), F32),
            pltpu.VMEM((count, columns, part), BF16),
            pltpu.VMEM((count, columns, part), BF16),
            pltpu.VMEM((columns, rows), F32),
            dma, dma((2,)),
        ] + [dma((count,))] * 10,
        compiler_params=pltpu.CompilerParams(
            collective_id=0, has_side_effects=True, vmem_limit_bytes=60 * 1024 * 1024
        ),
    )(
        genotypes, coefficients, to_time, later, earlier, to_id, mask, kept, kept_time,
        step_size[:, None], penalty[:, None],
    )


def solution(mesh):
    placed = (
        P("samp", "var"),
        P("pheno", "var"),
        P(("pheno", "samp")),
        P(("pheno", "samp")),
        P(("pheno", "samp")),
        P(),
        P(),
    )
    return jax.shard_map(
        local,
        mesh=mesh,
        in_specs=placed,
        out_specs=(P("pheno", "var"), P("pheno", "samp")),
        check_vma=False,
    )
```

time: 640 us -> 182 us (0.28)
  waiting for transfers between devices: 281 us -> 0.01 us
  blocking collectives: 162 us -> 0 us
  Pallas kernels: 0 us -> 149 us
  local copies, waits for them, and re-layouts: 58.1 us -> 5.05 us
  matrix products: 41.3 us -> 0 us
  other arithmetic: 51.5 us -> 13.6 us
  between operations: 15.9 us -> 0.7 us
  starting transfers between devices: 25.8 us -> 12.1 us
    psum x6 -> x0, waiting for transfers between devices: 269 us -> none  [the longest x3 231 us: local(): gradient = lax.psum(grad_partial, 'samp') * scale_samples]
    pallas_call x0 -> x1, Pallas kernels: none -> 149 us  [local(): pl.pallas_call(functools.partial(path_kernel, count, 1.0 / math.sqrt(VARS...]
    unnamed x7 -> x0, blocking collectives: 141 us -> none
    dot_general x6 -> x0, matrix products: 41.3 us -> none  [the longest x3 22.1 us: local(): lax.dot_general(coef_low, genotypes, (((1,), (1,)), ((), ())), preferred_...]
    gather x14 -> x0, local copies, waits for them, and re-layouts: 28.5 us -> none  [the longest x3 5.83 us: local(): returning = score_time[:, sorted_ids]]
    another operation x18 -> x0, other arithmetic: 23.7 us -> none
    all_to_all x2 -> x0, blocking collectives: 20.5 us -> none  [local(): lax.all_to_all(returning, 'samp', split_axis=1, concat_axis=1, tiled=True)]
    sort x4 -> x0, other arithmetic: 17.5 us -> none  [the longest x1 4.37 us: local(): send_order = jnp.argsort(owner_mine, stable=True)]
  transfers between devices with their start and end apart: 10 -> 2, of which waited for: 8 -> 0; matrix products, arithmetic and copies ran while one was open for 7% -> 5% of each run, Pallas kernels for 0% -> 0%
where the time goes in v1:
time: 182 us; the launch traced here: 181 us
  Pallas kernels  149 us (82%)
  other arithmetic  13.6 us (7%)
  starting transfers between devices  12.1 us (7%)
  local copies, waits for them, and re-layouts  5.05 us (3%)
    pallas_call x1, Pallas kernels, local(): pl.pallas_call(functools.partial(path_kernel, count, 1.0 / math.sqrt(VARS...  149 us
    all_to_all x1, starting transfers between devices, local(): lax.all_to_all(place_of.reshape(count, width), 'samp', 0, 0, tiled=True)  6.05 us
    all_to_all x1, starting transfers between devices, local(): lax.all_to_all(code_out.reshape(count, width), 'samp', 0, 0, tiled=True)  6 us
    unnamed x8, local copies, waits for them, and re-layouts  3.67 us
  transfers between devices with their start and end apart: 2, of which 0 were waited for; matrix products, arithmetic and copies ran while one was open for 5% of the time, Pallas kernels for 0%

profile of v1, /device:TPU:24, one launch (start us, length us, event | category | flops | bytes accessed | tf_op | source)
XLA Modules:
  0.0 180.8 jit_solution(11032637139972061841)
XLA Ops:
  0.6 0.0 copy-start.1
  0.6 0.0 copy-start.2
  0.6 0.7 add_select_fusion.5
  1.4 0.2 convert_reduce_fusion
  1.6 0.7 add_select_fusion.4
  2.3 1.3 select_reduce_fusion.2
  3.6 6.1 %all-to-all-start = ((s32[8,1,128]{2,1,0:T(1,128)}), s32[8,1,128]{2,1,0:T(1,128)S(1)}, u32[]{:S(2)}, u32[]{:S(2)}) async-start(s32[8,1,128]{2,1,0:T(1,128)} %bitcast), calls=%async_computation | async-start | bytes 8192 | tf_op jit(solution)/shard_map/all_to_all | solution.py:237
  9.7 0.8 fusion.22
  10.4 1.4 compare_convert_fusion.mask
  11.8 0.0 copy-start
  11.8 1.4 fusion.5.earlier
  13.2 1.4 fusion.later
  14.6 0.0 copy-done.1
  14.6 0.7 copy.12.penalty
  15.3 0.0 copy-done.2
  15.3 0.7 copy.11.step_size
  16.0 0.0 all-to-all-done
  16.0 1.2 select_reduce_fusion.1
  17.2 6.0 %all-to-all-start.1 = ((s32[8,1,128]{2,1,0:T(1,128)}), s32[8,1,128]{2,1,0:T(1,128)S(1)}, u32[]{:S(2)}, u32[]{:S(2)}) async-start(s32[8,1,128]{2,1,0:T(1,128)} %bitcast.2), calls=%async_computation.1 | async-start | bytes 8192 | tf_op jit(solution)/shard_map/all_to_all | solution.py:241
  23.2 1.7 fusion.2.to_id
  24.9 1.6 fusion.4.to_time
  26.6 0.0 all-to-all-done.1
  26.6 0.3 select_reduce_fusion
  26.9 0.0 copy-done
  26.9 0.8 compare_select_fusion.1
  27.7 149.4 %shard_map.86 = (f32[32,8192]{1,0:T(8,128)}, bf16[32,576]{1,0:T(8,128)(2,1)}) custom-call(bf16[576,8192]{1,0:T(8,128)(2,1)} %geno.1, f32[32,8192]{1,0:T(8,128)} %coef_in.1, bf16[576,1024]{1,0:T(8,128)(2,1)} %fusion.4.to_time, bf16[1024,576]{1,0:T(8,128)(2,1)} %fusion.later, bf16[576,1024]{1,0:T(8,128)(2,1)} %fusion.5.earlier, ...), custom_call_target="tpu_custom_call" | custom-call | tf_op jit(solution)/shard_map/pallas_call | solution.py:263
  177.1 2.3 %copy.15 = f32[32,8192]{1,0:T(8,128)} copy(f32[32,8192]{1,0:T(8,128)} %get-tuple-element.18) | data formatting | bytes 2097152
  179.4 1.4 copy.16
  (7 shorter events, 0.0 us)
Async XLA Ops:
  0.6 14.0 %copy-start.1 = (f32[32]{0:T(128)S(1)}, f32[32]{0:T(128)}, u32[]{:S(2)}) copy-start(f32[32]{0:T(128)} %param.12) | copy-start | bytes 388
  0.6 14.6 %copy-start.2 = (f32[32]{0:T(128)S(1)}, f32[32]{0:T(128)}, u32[]{:S(2)}) copy-start(f32[32]{0:T(128)} %param.13) | copy-start | bytes 388
  3.6 12.4 %all-to-all-start = ((s32[8,1,128]{2,1,0:T(1,128)}), s32[8,1,128]{2,1,0:T(1,128)S(1)}, u32[]{:S(2)}, u32[]{:S(2)}) async-start(s32[8,1,128]{2,1,0:T(1,128)} %bitcast), calls=%async_computation | async-start | bytes 8192 | tf_op jit(solution)/shard_map/all_to_all | solution.py:237
  11.8 15.1 %copy-start = (s32[576]{0:T(1024)S(1)}, s32[576]{0:T(1024)}, u32[]{:S(2)}) copy-start(s32[576]{0:T(1024)} %param.10) | copy-start | bytes 6916
  17.2 9.4 %all-to-all-start.1 = ((s32[8,1,128]{2,1,0:T(1,128)}), s32[8,1,128]{2,1,0:T(1,128)S(1)}, u32[]{:S(2)}, u32[]{:S(2)}) async-start(s32[8,1,128]{2,1,0:T(1,128)} %bitcast.2), calls=%async_computation.1 | async-start | bytes 8192 | tf_op jit(solution)/shard_map/all_to_all | solution.py:241

commit v2 on v1

--- a/solution.py
+++ b/solution.py
@@ -30,6 +30,16 @@
     return jnp.concatenate([high, low], axis=0)
 
 
+def across(left, right):
+    return lax.dot_general(left, right, (((1,), (1,)), ((), ())), preferred_element_type=F32)
+
+
+def across2(value, matrix):
+    rows = value.shape[0]
+    both = across(halves(value), matrix)
+    return both[:rows] + both[rows:]
+
+
 def dot2(value, matrix):
     rows = value.shape[0]
     both = jnp.dot(halves(value), matrix, preferred_element_type=F32)
@@ -38,23 +48,33 @@
 
 def path_kernel(
     count, scale_vars, scale_samples,
-    geno, coef_in, to_time, later, earlier, to_id, mask, kept, kept_time, step_size, penalty,
+    geno_in, coef_in, labels, place_out, reach, back, spot, step_size, penalty,
     coef_out, score_out,
+    geno, to_time, later, earlier, to_id, mask, kept, kept_time, place_in, code_out, code_in,
     low, shard, half_send, half_recv, out_a, in_a, out_b, in_b, out_g, in_g, pred,
-    half_ss, half_rs, a_ss, a_rs, b_ss, b_rs, g_ss, g_rs, c_ss, c_rs, f_ss, f_rs,
+    load_sem, p_ss, p_rs, l_ss, l_rs, fwd_ss, last_ss, half_ss, half_rs, a_ss, a_rs, b_ss, b_rs, g_ss, g_rs, c_ss, c_rs, f_ss, f_rs,
 ):
     me = lax.axis_index("samp")
     var = lax.axis_index("var")
     columns, variants = coef_in.shape
     rows = geno.shape[0]
     part = variants // count
-    width = later.shape[0] // count
+    width = later.shape[1] // count
+    share = rows // count
+    half = count // 2
+    load = pltpu.make_async_copy(geno_in, geno, load_sem)
+    load.start()
 
     def peer(step):
         return lax.rem(me + step, count)
 
     def piece(owner):
         return pl.ds(pl.multiple_of(owner * part, part), part)
+
+    side = 1 - 2 * lax.rem(me, 2)
+
+    def down(step):
+        return lax.rem(me + 2 * step, count)
 
     def slots(owner):
         return pl.ds(pl.multiple_of(owner * width, width), width)
@@ -78,6 +98,16 @@
             device_id_type=MESH,
         )
 
+    def relay(source, target, ssem, rsem, owner):
+        return pltpu.make_async_remote_copy(
+            src_ref=source,
+            dst_ref=target,
+            send_sem=ssem.at[owner],
+            recv_sem=rsem.at[owner],
+            device_id={"samp": me + side},
+            device_id_type=MESH,
+        )
+
     def arrive(source, target, ssem, rsem, owner):
         pltpu.make_async_remote_copy(
             src_ref=source,
@@ -88,31 +118,92 @@
             device_id_type=MESH,
         ).wait_recv()
 
+    def push_p(step):
+        owner = peer(step + 1)
+        send(place_out.at[owner], place_in.at[me], p_ss, p_rs, owner).start()
+    each(count - 1, push_p)
+
+    column_fold = lax.rem(lax.broadcasted_iota(jnp.int32, (columns, rows), 0), FOLDS).astype(F32)
+    mask[...] = jnp.where(labels[0:1, :] != column_fold, 1.0, 0.0)
+    kept[...] = mask[...] * labels[1:2, :]
+    ranks = lax.broadcasted_iota(jnp.int32, (rows, width), 0)
+    lane = lax.broadcasted_iota(jnp.int32, (rows, width), 1)
+    for owner in range(count):
+        span = slice(owner * width, (owner + 1) * width)
+        later[:, span] = jnp.where(reach[owner] >= ranks, 1.0, 0.0).astype(BF16)
+        earlier[:, span] = jnp.where(back[owner] >= ranks, 1.0, 0.0).astype(BF16)
+
+    place_in[me] = place_out[me]
+    block = jnp.zeros((rows, width), jnp.int32)
+    def land_p(step):
+        owner = peer(step + 1)
+        arrive(place_out.at[owner], place_in.at[owner], p_ss, p_rs, owner)
+        send(place_out.at[owner], place_in.at[me], p_ss, p_rs, owner).wait_send()
+    each(count - 1, land_p)
+    for owner in range(1, count):
+        block += jnp.where(place_in[owner] == ranks, owner, 0)
+    block = jnp.broadcast_to(jnp.sum(block, axis=1, keepdims=True), (rows, width))
+    in_totals = (lane - share) == block
+    for owner in range(count):
+        span = slice(owner * width, (owner + 1) * width)
+        hit = place_in[owner] == ranks
+        to_time[:, span] = jnp.where(hit | in_totals, 1.0, 0.0).astype(BF16)
+        to_id[:, span] = jnp.where(hit | ((lane == share) & (block > owner)), 1.0, 0.0).astype(BF16)
+    spread = jnp.dot(labels[...].astype(BF16), to_time[...], preferred_element_type=F32)
+    for owner in range(count):
+        code_out[owner] = spread[:, owner * width:(owner + 1) * width]
+
+    def push_l(step):
+        owner = peer(step + 1)
+        send(code_out.at[owner], code_in.at[me], l_ss, l_rs, owner).start()
+    each(count - 1, push_l)
+    code_in[me] = code_out[me]
+
+    def land_l(step):
+        owner = peer(step + 1)
+        arrive(code_out.at[owner], code_in.at[owner], l_ss, l_rs, owner)
+        send(code_out.at[owner], code_in.at[me], l_ss, l_rs, owner).wait_send()
+    each(count - 1, land_l)
+    labels_time = jnp.zeros((labels.shape[0], rows), F32)
+    for owner in range(count):
+        labels_time += across(
+            code_in[owner].astype(BF16), jnp.where(spot[owner] == ranks, 1.0, 0.0).astype(BF16)
+        )
+    kept_time[...] = jnp.where(labels_time[0:1, :] != column_fold, 1.0, 0.0) * labels_time[1:2, :]
+
     def fill(step):
         low[step] = coef_in[:, piece(step)].astype(BF16)
 
     each(count, fill)
     shard[...] = coef_in[:, piece(me)]
+    load.wait()
 
     def one_step(turn, carry):
         pred[...] = jnp.zeros_like(pred)
 
-        def add_part(step):
-            owner = peer(step)
-            if not (isinstance(step, int) and step == 0):
-                @pl.when(turn > 0)
-                def _():
-                    if isinstance(step, int):
-                        arrive(low.at[owner], low.at[owner], c_ss, c_rs, owner)
-                    else:
-                        @pl.when(step > 0)
-                        def _():
-                            arrive(low.at[owner], low.at[owner], c_ss, c_rs, owner)
-            pred[...] += lax.dot_general(
-                low[owner], geno[:, piece(owner)], (((1,), (1,)), ((), ())), preferred_element_type=F32
-            )
-
-        each(count, add_part)
+        def add_part(owner):
+            pred[...] += across(low[owner], geno[:, piece(owner)])
+
+        def add_down(step):
+            owner = down(step + 1)
+
+            @pl.when(turn > 0)
+            def _():
+                arrive(low.at[owner], low.at[owner], c_ss, c_rs, owner)
+                relay(low.at[owner], low.at[owner], fwd_ss, c_rs, owner).start()
+            add_part(owner)
+
+        def add_side(step):
+            owner = down(step) + side
+
+            @pl.when(turn > 0)
+            def _():
+                arrive(low.at[owner], low.at[owner], c_ss, c_rs, owner)
+            add_part(owner)
+
+        add_part(me)
+        each(half - 1, add_down)
+        each(half, add_side)
         half_send[...] = pred[...]
         slot = lax.rem(turn, 2)
         swap = pltpu.make_async_remote_copy(
@@ -125,9 +216,11 @@
         @pl.when(turn > 0)
         def _():
             def drained(step):
-                owner = peer(step + 1)
+                owner = down(step + 1)
                 send(low.at[me], low.at[me], c_ss, c_rs, owner).wait_send()
-            each(count - 1, drained)
+                relay(low.at[owner], low.at[owner], fwd_ss, c_rs, owner).wait_send()
+            each(half - 1, drained)
+            send(low.at[me], low.at[me], c_ss, c_rs, me + side).wait_send()
 
         weight = mask[...] * jnp.exp((half_send[...] + half_recv[slot]) * scale_vars)
         pred[...] = weight
@@ -139,11 +232,11 @@
             owner = peer(step + 1)
             send(out_a.at[owner], in_a.at[me], a_ss, a_rs, owner).start()
         each(count - 1, push_a)
-        risk = dot2(out_a[me], later[slots(me), :])
+        risk = across2(out_a[me], later[:, slots(me)])
         for step in range(count - 1):
             owner = peer(step + 1)
             arrive(out_a.at[owner], in_a.at[owner], a_ss, a_rs, owner)
-            risk += dot2(in_a[owner], later[slots(owner), :])
+            risk += across2(in_a[owner], later[:, slots(owner)])
         events = kept_time[...]
         ratio = events / jnp.where(events > 0, risk, 1.0)
         spread = dot2(ratio, earlier[...])
@@ -154,11 +247,11 @@
             owner = peer(step + 1)
             send(out_b.at[owner], in_b.at[me], b_ss, b_rs, owner).start()
         each(count - 1, push_b)
-        hazard = dot2(out_b[me], to_id[slots(me), :])
+        hazard = across2(out_b[me], to_id[:, slots(me)])
         for step in range(count - 1):
             owner = peer(step + 1)
             arrive(out_b.at[owner], in_b.at[owner], b_ss, b_rs, owner)
-            hazard += dot2(in_b[owner], to_id[slots(owner), :])
+            hazard += across2(in_b[owner], to_id[:, slots(owner)])
         score_out[...] = (pred[...] * hazard - kept[...]).astype(BF16)
 
         def push_g(step):
@@ -190,9 +283,10 @@
             low[me] = fresh.astype(BF16)
 
             def push_c(step):
-                owner = peer(step + 1)
+                owner = down(step + 1)
                 send(low.at[me], low.at[me], c_ss, c_rs, owner).start()
-            each(count - 1, push_c)
+            each(half - 1, push_c)
+            send(low.at[me], low.at[me], c_ss, c_rs, me + side).start()
 
         each(count - 1, drained_all)
         return carry
@@ -202,15 +296,28 @@
     coef_out[:, piece(me)] = shard[...]
 
     def push_f(step):
-        owner = peer(step + 1)
+        owner = down(step + 1)
         send(shard, coef_out.at[:, piece(me)], f_ss, f_rs, owner).start()
-    each(count - 1, push_f)
+    each(half - 1, push_f)
+    send(shard, coef_out.at[:, piece(me)], f_ss, f_rs, me + side).start()
+
+    def pass_f(step):
+        owner = down(step + 1)
+        arrive(shard, coef_out.at[:, piece(owner)], f_ss, f_rs, owner)
+        relay(coef_out.at[:, piece(owner)], coef_out.at[:, piece(owner)], last_ss, f_rs, owner).start()
+    each(half - 1, pass_f)
 
     def land_f(step):
-        owner = peer(step + 1)
+        owner = down(step) + side
         arrive(shard, coef_out.at[:, piece(owner)], f_ss, f_rs, owner)
+    each(half, land_f)
+
+    def done_f(step):
+        owner = down(step + 1)
         send(shard, coef_out.at[:, piece(me)], f_ss, f_rs, owner).wait_send()
-    each(count - 1, land_f)
+        relay(coef_out.at[:, piece(owner)], coef_out.at[:, piece(owner)], last_ss, f_rs, owner).wait_send()
+    each(half - 1, done_f)
+    send(shard, coef_out.at[:, piece(me)], f_ss, f_rs, me + side).wait_send()
 
 
 def local(genotypes, coefficients, time_order, fold_label, event_flag, penalty, step_size):
@@ -226,7 +333,6 @@
     ranks = jnp.arange(rows, dtype=jnp.int32)
     slot_all = jnp.arange(total, dtype=jnp.int32)
     lane = slot_all % width
-    group = slot_all // width
     owner = time_order // rows
     place = time_order % rows
     same = (owner[:, None] == owner[None, :]) & (ranks[:, None] < ranks[None, :])
@@ -234,29 +340,13 @@
     match = key[:, None] == slot_all[None, :]
     rank_of = jnp.max(jnp.where(match, ranks[:, None], -1), axis=0)
     place_of = jnp.max(jnp.where(match, place[:, None], -1), axis=0)
-    place_in = lax.all_to_all(place_of.reshape(count, width), "samp", 0, 0, tiled=True).reshape(total)
-    match_id = place_in[None, :] == ranks[:, None]
-    code = fold_label * 2 + event_flag
-    code_out = jnp.sum(jnp.where(match_id, code[:, None], 0), axis=0)
-    code_in = lax.all_to_all(code_out.reshape(count, width), "samp", 0, 0, tiled=True).reshape(total)
-    code_time = jnp.sum(jnp.where(rank_of[None, :] == ranks[:, None], code_in[None, :], 0), axis=1)
-    block = jnp.sum(jnp.where(match_id, group[None, :], 0), axis=1)
-
     in_totals = (lane >= share) & (lane < share + count)
-    to_time = (match_id | (in_totals[None, :] & ((lane - share)[None, :] == block[:, None]))).astype(BF16)
-    reach = jnp.where(lane < share, rank_of, jnp.where(in_totals & (lane - share > me), rows, -1))
-    later = (reach[:, None] >= ranks[None, :]).astype(BF16)
-    back = jnp.where(lane < share, rank_of, jnp.where(lane == share, rows, -1))
-    earlier = (ranks[:, None] <= back[None, :]).astype(BF16)
-    to_id = (
-        (place_in[:, None] == ranks[None, :])
-        | ((lane == share)[:, None] & (group[:, None] < block[None, :]))
-    ).astype(BF16)
-
-    column_fold = jnp.arange(columns, dtype=jnp.int32) % FOLDS
-    mask = (fold_label[None, :] != column_fold[:, None]).astype(F32)
-    kept = mask * event_flag.astype(F32)[None, :]
-    kept_time = ((code_time // 2)[None, :] != column_fold[:, None]).astype(F32) * (code_time % 2).astype(F32)[None, :]
+    spot = jnp.where(lane < share, rank_of, -1)
+    reach = jnp.where(in_totals & (lane - share > me), rows, spot)
+    back = jnp.where(lane == share, rows, spot)
+    labels = jnp.stack([fold_label, event_flag]).astype(F32)
+    labels = jnp.concatenate([labels, jnp.zeros((6, rows), F32)])
+    place_of, reach, back, spot = (value.reshape(count, 1, width) for value in (place_of, reach, back, spot))
 
     vmem = pl.BlockSpec(memory_space=pltpu.VMEM)
     dma = pltpu.SemaphoreType.DMA
@@ -266,9 +356,20 @@
             jax.ShapeDtypeStruct((columns, variants), F32),
             jax.ShapeDtypeStruct((columns, rows), BF16),
         ),
-        in_specs=[vmem] * 11,
+        in_specs=[pl.BlockSpec(memory_space=pl.ANY)] + [vmem] * 8,
         out_specs=(vmem, vmem),
         scratch_shapes=[
+            pltpu.VMEM((rows, variants), BF16),
+            pltpu.VMEM((rows, total), BF16),
+            pltpu.VMEM((rows, total), BF16),
+            pltpu.VMEM((rows, total), BF16),
+            pltpu.VMEM((rows, total), BF16),
+            pltpu.VMEM((columns, rows), F32),
+            pltpu.VMEM((columns, rows), F32),
+            pltpu.VMEM((columns, rows), F32),
+            pltpu.VMEM((count, 1, width), jnp.int32),
+            pltpu.VMEM((count, 8, width), F32),
+            pltpu.VMEM((count, 8, width), F32),
             pltpu.VMEM((count, columns, part), BF16),
             pltpu.VMEM((columns, part), F32),
             pltpu.VMEM((columns, rows), F32),
@@ -280,13 +381,15 @@
             pltpu.VMEM((count, columns, part), BF16),
             pltpu.VMEM((count, columns, part), BF16),
             pltpu.VMEM((columns, rows), F32),
+            dma,
+        ] + [dma((count,))] * 6 + [
             dma, dma((2,)),
         ] + [dma((count,))] * 10,
         compiler_params=pltpu.CompilerParams(
             collective_id=0, has_side_effects=True, vmem_limit_bytes=60 * 1024 * 1024
         ),
     )(
-        genotypes, coefficients, to_time, later, earlier, to_id, mask, kept, kept_time,
+        genotypes, coefficients, labels, place_of, reach, back, spot,
         step_size[:, None], penalty[:, None],
     )
 

time: 182 us -> 161 us (0.88)
  starting transfers between devices: 12.1 us -> 0 us
  other arithmetic: 13.6 us -> 4.13 us
  local copies, waits for them, and re-layouts: 5.05 us -> 8.33 us
  Pallas kernels: 149 us -> 147 us
    all_to_all x2 -> x0, starting transfers between devices: 12.1 us -> none  [the longest x1 6.05 us: local(): lax.all_to_all(place_of.reshape(count, width), 'samp', 0, 0, tiled=True)]
    convert_element_type x6 -> x1, other arithmetic: 8.29 us -> 0.01 us  [local(): labels = jnp.stack([fold_label, event_flag]).astype(F32)]
    pallas_call x1, Pallas kernels: 149 us -> 147 us  [local(): pl.pallas_call(functools.partial(path_kernel, count, 1.0 / math.sqrt(VARS...]
    unnamed x8 -> x4, local copies, waits for them, and re-layouts: 3.67 us -> 3.67 us
  transfers between devices with their start and end apart: 2 -> 0, of which waited for: 0 -> 0; matrix products, arithmetic and copies ran while one was open for 5% -> 0% of each run, Pallas kernels for 0% -> 0%
where the time goes in v2:
time: 161 us; the launch traced here: 160 us
  Pallas kernels  147 us (91%)
  local copies, waits for them, and re-layouts  8.33 us (5%)
  other arithmetic  4.13 us (3%)
    pallas_call x1, Pallas kernels, local(): pl.pallas_call(functools.partial(path_kernel, count, 1.0 / math.sqrt(VARS...  147 us
    unnamed x4, local copies, waits for them, and re-layouts  3.67 us

profile of v2, /device:TPU:24, one launch (start us, length us, event | category | flops | bytes accessed | tf_op | source)
XLA Modules:
  0.0 159.7 jit_solution(9876700394024508611)
XLA Ops:
  0.6 0.7 stack.9
  1.3 0.7 stack.10
  2.0 0.7 add_select_fusion.1
  2.7 0.2 convert_reduce_fusion
  3.0 0.7 add_select_fusion
  3.7 1.3 select_reduce_fusion
  4.9 0.6 compare_select_fusion.2
  5.5 0.0 copy-start
  5.5 0.6 and_select_fusion.reach
  6.2 0.6 concatenate.3.labels
  6.8 1.3 copy.12.penalty
  8.1 1.3 copy.11.step_size
  9.4 0.0 copy-done
  9.4 146.5 %shard_map.86 = (f32[32,8192]{1,0:T(8,128)}, bf16[32,576]{1,0:T(8,128)(2,1)}) custom-call(bf16[576,8192]{1,0:T(8,128)(2,1)} %geno_in.1, f32[32,8192]{1,0:T(8,128)} %coef_in.1, f32[8,576]{1,0:T(8,128)} %concatenate.3.labels, s32[8,1,128]{2,1,0:T(1,128)} %bitcast.4, s32[8,1,128]{2,1,0:T(1,128)} %and_select_fusion.reach, s32[8,1,128]{2,1,0:T(1,128)} %get-tuple-element.4.back, ...), custom_call_target="tpu_custom_call" | custom-call | tf_op jit(solution)/shard_map/pallas_call | solution.py:353
  156.0 2.3 %copy.15 = f32[32,8192]{1,0:T(8,128)} copy(f32[32,8192]{1,0:T(8,128)} %get-tuple-element.10) | data formatting | bytes 2097152
  158.3 1.4 copy.16
  (1 shorter events, 0.0 us)
Async XLA Ops:
  5.5 3.9 %copy-start = (s32[8,1,128]{2,1,0:T(1,128)}, s32[8,1,128]{2,1,0:T(1,128)S(1)}, u32[]{:S(2)}) copy-start(s32[8,1,128]{2,1,0:T(1,128)S(1)} %get-tuple-element.5.spot) | copy-start | bytes 12292

commit v3 on v2

--- a/solution.py
+++ b/solution.py
@@ -12,6 +12,7 @@
 FOLDS = 8
 ITERS = 3
 MESH = pl.DeviceIdType.MESH
+CUTS = 4
 F32 = jnp.float32
 BF16 = jnp.bfloat16
 
@@ -48,7 +49,7 @@
 
 def path_kernel(
     count, scale_vars, scale_samples,
-    geno_in, coef_in, labels, place_out, reach, back, spot, step_size, penalty,
+    geno_in, coef_in, fold_row, event_row, place_out, reach, back, spot, step_row, penalty_row,
     coef_out, score_out,
     geno, to_time, later, earlier, to_id, mask, kept, kept_time, place_in, code_out, code_in,
     low, shard, half_send, half_recv, out_a, in_a, out_b, in_b, out_g, in_g, pred,
@@ -76,6 +77,57 @@
     def down(step):
         return lax.rem(me + 2 * step, count)
 
+    cuts = min(CUTS, part // 128)
+    cut = part // cuts
+
+    def bit(owner, number):
+        return low.at[owner, :, pl.ds(number * cut, cut)]
+
+    def wide(owner, number):
+        return coef_out.at[:, pl.ds(pl.multiple_of(owner * part + number * cut, cut), cut)]
+
+    def send_to(spot_of, ssem, rsem, number, owner):
+        return pltpu.make_async_remote_copy(
+            src_ref=spot_of(me, number), dst_ref=spot_of(me, number),
+            send_sem=ssem.at[owner, number], recv_sem=rsem.at[me, number],
+            device_id={"samp": owner}, device_id_type=MESH,
+        )
+
+    def pass_on(spot_of, ssem, rsem, number, owner):
+        return pltpu.make_async_remote_copy(
+            src_ref=spot_of(owner, number), dst_ref=spot_of(owner, number),
+            send_sem=ssem.at[owner, number], recv_sem=rsem.at[owner, number],
+            device_id={"samp": me + side}, device_id_type=MESH,
+        )
+
+    def spread_out(spot_of, ssem, rsem):
+        for number in range(cuts):
+            def go(step):
+                send_to(spot_of, ssem, rsem, number, down(step + 1)).start()
+            send_to(spot_of, ssem, rsem, number, me + side).start()
+            each(half - 1, go)
+
+    def relay_all(spot_of, ssem, rsem):
+        for number in range(cuts):
+            def go(step):
+                copy = pass_on(spot_of, ssem, rsem, number, down(step + 1))
+                copy.wait_recv()
+                copy.start()
+            each(half - 1, go)
+
+    def land(spot_of, ssem, rsem, owner):
+        for number in range(cuts):
+            pass_on(spot_of, ssem, rsem, number, owner).wait_recv()
+
+    def settle(spot_of, ssem, fsem, rsem):
+        for number in range(cuts):
+            def go(step):
+                owner = down(step + 1)
+                send_to(spot_of, ssem, rsem, number, owner).wait_send()
+                pass_on(spot_of, fsem, rsem, number, owner).wait_send()
+            each(half - 1, go)
+            send_to(spot_of, ssem, rsem, number, me + side).wait_send()
+
     def slots(owner):
         return pl.ds(pl.multiple_of(owner * width, width), width)
 
@@ -98,16 +150,6 @@
             device_id_type=MESH,
         )
 
-    def relay(source, target, ssem, rsem, owner):
-        return pltpu.make_async_remote_copy(
-            src_ref=source,
-            dst_ref=target,
-            send_sem=ssem.at[owner],
-            recv_sem=rsem.at[owner],
-            device_id={"samp": me + side},
-            device_id_type=MESH,
-        )
-
     def arrive(source, target, ssem, rsem, owner):
         pltpu.make_async_remote_copy(
             src_ref=source,
@@ -123,6 +165,13 @@
         send(place_out.at[owner], place_in.at[me], p_ss, p_rs, owner).start()
     each(count - 1, push_p)
 
+    line = lax.broadcasted_iota(jnp.int32, (8, rows), 0)
+    labels = jnp.where(line == 0, fold_row[...], jnp.where(line == 1, event_row[...], 0)).astype(F32)
+    same = lax.broadcasted_iota(jnp.int32, (columns, columns), 0) == lax.broadcasted_iota(
+        jnp.int32, (columns, columns), 1
+    )
+    pace = jnp.sum(jnp.where(same, step_row[...], 0.0), axis=1, keepdims=True)
+    threshold = pace * jnp.sum(jnp.where(same, penalty_row[...], 0.0), axis=1, keepdims=True)
     column_fold = lax.rem(lax.broadcasted_iota(jnp.int32, (columns, rows), 0), FOLDS).astype(F32)
     mask[...] = jnp.where(labels[0:1, :] != column_fold, 1.0, 0.0)
     kept[...] = mask[...] * labels[1:2, :]
@@ -149,7 +198,7 @@
         hit = place_in[owner] == ranks
         to_time[:, span] = jnp.where(hit | in_totals, 1.0, 0.0).astype(BF16)
         to_id[:, span] = jnp.where(hit | ((lane == share) & (block > owner)), 1.0, 0.0).astype(BF16)
-    spread = jnp.dot(labels[...].astype(BF16), to_time[...], preferred_element_type=F32)
+    spread = jnp.dot(labels.astype(BF16), to_time[...], preferred_element_type=F32)
     for owner in range(count):
         code_out[owner] = spread[:, owner * width:(owner + 1) * width]
 
@@ -185,23 +234,21 @@
             pred[...] += across(low[owner], geno[:, piece(owner)])
 
         def add_down(step):
-            owner = down(step + 1)
+            add_part(down(step + 1))
+
+        def add_side(step):
+            owner = down(step) + side
 
             @pl.when(turn > 0)
             def _():
-                arrive(low.at[owner], low.at[owner], c_ss, c_rs, owner)
-                relay(low.at[owner], low.at[owner], fwd_ss, c_rs, owner).start()
+                land(bit, c_ss, c_rs, owner)
             add_part(owner)
 
-        def add_side(step):
-            owner = down(step) + side
-
-            @pl.when(turn > 0)
-            def _():
-                arrive(low.at[owner], low.at[owner], c_ss, c_rs, owner)
-            add_part(owner)
-
         add_part(me)
+
+        @pl.when(turn > 0)
+        def _():
+            relay_all(bit, fwd_ss, c_rs)
         each(half - 1, add_down)
         each(half, add_side)
         half_send[...] = pred[...]
@@ -215,12 +262,7 @@
 
         @pl.when(turn > 0)
         def _():
-            def drained(step):
-                owner = down(step + 1)
-                send(low.at[me], low.at[me], c_ss, c_rs, owner).wait_send()
-                relay(low.at[owner], low.at[owner], fwd_ss, c_rs, owner).wait_send()
-            each(half - 1, drained)
-            send(low.at[me], low.at[me], c_ss, c_rs, me + side).wait_send()
+            settle(bit, c_ss, fwd_ss, c_rs)
 
         weight = mask[...] * jnp.exp((half_send[...] + half_recv[slot]) * scale_vars)
         pred[...] = weight
@@ -266,9 +308,8 @@
             owner = peer(count - 1 - step)
             arrive(out_g.at[owner], in_g.at[owner], g_ss, g_rs, owner)
             total += in_g[owner].astype(F32)
-        pace = step_size[...]
         stepped = shard[...] - pace * (total * scale_samples)
-        shrunk = jnp.maximum(jnp.abs(stepped) - pace * penalty[...], 0.0)
+        shrunk = jnp.maximum(jnp.abs(stepped) - threshold, 0.0)
         fresh = jnp.where(stepped > 0, shrunk, -shrunk)
         shard[...] = fresh
 
@@ -282,11 +323,7 @@
         def _():
             low[me] = fresh.astype(BF16)
 
-            def push_c(step):
-                owner = down(step + 1)
-                send(low.at[me], low.at[me], c_ss, c_rs, owner).start()
-            each(half - 1, push_c)
-            send(low.at[me], low.at[me], c_ss, c_rs, me + side).start()
+            spread_out(bit, c_ss, c_rs)
 
         each(count - 1, drained_all)
         return carry
@@ -295,29 +332,13 @@
 
     coef_out[:, piece(me)] = shard[...]
 
-    def push_f(step):
-        owner = down(step + 1)
-        send(shard, coef_out.at[:, piece(me)], f_ss, f_rs, owner).start()
-    each(half - 1, push_f)
-    send(shard, coef_out.at[:, piece(me)], f_ss, f_rs, me + side).start()
-
-    def pass_f(step):
-        owner = down(step + 1)
-        arrive(shard, coef_out.at[:, piece(owner)], f_ss, f_rs, owner)
-        relay(coef_out.at[:, piece(owner)], coef_out.at[:, piece(owner)], last_ss, f_rs, owner).start()
-    each(half - 1, pass_f)
+    spread_out(wide, f_ss, f_rs)
+    relay_all(wide, last_ss, f_rs)
 
     def land_f(step):
-        owner = down(step) + side
-        arrive(shard, coef_out.at[:, piece(owner)], f_ss, f_rs, owner)
+        land(wide, f_ss, f_rs, down(step) + side)
     each(half, land_f)
-
-    def done_f(step):
-        owner = down(step + 1)
-        send(shard, coef_out.at[:, piece(me)], f_ss, f_rs, owner).wait_send()
-        relay(coef_out.at[:, piece(owner)], coef_out.at[:, piece(owner)], last_ss, f_rs, owner).wait_send()
-    each(half - 1, done_f)
-    send(shard, coef_out.at[:, piece(me)], f_ss, f_rs, me + side).wait_send()
+    settle(wide, f_ss, last_ss, f_rs)
 
 
 def local(genotypes, coefficients, time_order, fold_label, event_flag, penalty, step_size):
@@ -344,8 +365,6 @@
     spot = jnp.where(lane < share, rank_of, -1)
     reach = jnp.where(in_totals & (lane - share > me), rows, spot)
     back = jnp.where(lane == share, rows, spot)
-    labels = jnp.stack([fold_label, event_flag]).astype(F32)
-    labels = jnp.concatenate([labels, jnp.zeros((6, rows), F32)])
     place_of, reach, back, spot = (value.reshape(count, 1, width) for value in (place_of, reach, back, spot))
 
     vmem = pl.BlockSpec(memory_space=pltpu.VMEM)
@@ -356,7 +375,7 @@
             jax.ShapeDtypeStruct((columns, variants), F32),
             jax.ShapeDtypeStruct((columns, rows), BF16),
         ),
-        in_specs=[pl.BlockSpec(memory_space=pl.ANY)] + [vmem] * 8,
+        in_specs=[pl.BlockSpec(memory_space=pl.ANY)] + [vmem] * 9,
         out_specs=(vmem, vmem),
         scratch_shapes=[
             pltpu.VMEM((rows, variants), BF16),
@@ -382,15 +401,15 @@
             pltpu.VMEM((count, columns, part), BF16),
             pltpu.VMEM((columns, rows), F32),
             dma,
-        ] + [dma((count,))] * 6 + [
+        ] + [dma((count,))] * 4 + [dma((count, CUTS))] * 2 + [
             dma, dma((2,)),
-        ] + [dma((count,))] * 10,
+        ] + [dma((count,))] * 6 + [dma((count, CUTS))] * 4,
         compiler_params=pltpu.CompilerParams(
             collective_id=0, has_side_effects=True, vmem_limit_bytes=60 * 1024 * 1024
         ),
     )(
-        genotypes, coefficients, labels, place_of, reach, back, spot,
-        step_size[:, None], penalty[:, None],
+        genotypes, coefficients, fold_label[None], event_flag[None], place_of, reach, back, spot,
+        step_size[None], penalty[None],
     )
 
 

time: 161 us -> 155 us (0.963)
  Pallas kernels: 147 us -> 143 us
  local copies, waits for them, and re-layouts: 8.33 us -> 6.21 us
    pallas_call x1, Pallas kernels: 147 us -> 143 us  [local(): pl.pallas_call(functools.partial(path_kernel, count, 1.0 / math.sqrt(VARS...]
where the time goes in v3:
time: 155 us; the launch traced here: 154 us
  Pallas kernels  143 us (92%)
  local copies, waits for them, and re-layouts  6.21 us (4%)
  other arithmetic  4.11 us (3%)
    pallas_call x1, Pallas kernels, local(): pl.pallas_call(functools.partial(path_kernel, count, 1.0 / math.sqrt(VARS...  143 us
    unnamed x4, local copies, waits for them, and re-layouts  3.67 us

profile of v3, /device:TPU:24, one launch (start us, length us, event | category | flops | bytes accessed | tf_op | source)
XLA Modules:
  0.0 154.3 jit_solution(1356184662163474564)
XLA Ops:
  0.6 1.3 broadcast_in_dim.47.fold_row
  1.9 1.3 broadcast_in_dim.48.event_row
  3.2 0.7 add_select_fusion.1
  3.9 0.2 convert_reduce_fusion
  4.1 0.7 add_select_fusion
  4.8 1.3 select_reduce_fusion
  6.1 0.6 compare_select_fusion.2
  6.7 0.0 copy-start
  6.7 0.6 and_select_fusion.reach
  7.3 0.0 copy-done
  7.3 143.3 %shard_map.86 = (f32[32,8192]{1,0:T(8,128)}, bf16[32,576]{1,0:T(8,128)(2,1)}) custom-call(bf16[576,8192]{1,0:T(8,128)(2,1)} %geno_in.1, f32[32,8192]{1,0:T(8,128)} %coef_in.1, s32[1,576]{1,0:T(1,128)} %broadcast_in_dim.47.fold_row, s32[1,576]{1,0:T(1,128)} %broadcast_in_dim.48.event_row, s32[8,1,128]{2,1,0:T(1,128)} %bitcast.4, ...), custom_call_target="tpu_custom_call" | custom-call | tf_op jit(solution)/shard_map/pallas_call | solution.py:372
  150.6 2.3 %copy.11 = f32[32,8192]{1,0:T(8,128)} copy(f32[32,8192]{1,0:T(8,128)} %get-tuple-element.10) | data formatting | bytes 2097152
  152.9 1.4 copy.12
Async XLA Ops:
  6.7 0.6 copy-start

commit v4 on v3

--- a/solution.py
+++ b/solution.py
@@ -12,7 +12,7 @@
 FOLDS = 8
 ITERS = 3
 MESH = pl.DeviceIdType.MESH
-CUTS = 4
+CUTS = 8
 F32 = jnp.float32
 BF16 = jnp.bfloat16
 
@@ -49,10 +49,10 @@
 
 def path_kernel(
     count, scale_vars, scale_samples,
-    geno_in, coef_in, fold_row, event_row, place_out, reach, back, spot, step_row, penalty_row,
+    geno_in, coef_in, code_row, place_out, reach, back, spot, step_row, penalty_row,
     coef_out, score_out,
     geno, to_time, later, earlier, to_id, mask, kept, kept_time, place_in, code_out, code_in,
-    low, shard, half_send, half_recv, out_a, in_a, out_b, in_b, out_g, in_g, pred,
+    low, shard, half_send, half_recv, out_a, in_a, out_b, in_b, out_g, in_g, pred, held, s_ss, s_rs,
     load_sem, p_ss, p_rs, l_ss, l_rs, fwd_ss, last_ss, half_ss, half_rs, a_ss, a_rs, b_ss, b_rs, g_ss, g_rs, c_ss, c_rs, f_ss, f_rs,
 ):
     me = lax.axis_index("samp")
@@ -63,6 +63,9 @@
     width = later.shape[1] // count
     share = rows // count
     half = count // 2
+    few = columns // 2
+    mine = pl.ds(pl.multiple_of(var * few, few), few)
+    theirs = pl.ds(pl.multiple_of((1 - var) * few, few), few)
     load = pltpu.make_async_copy(geno_in, geno, load_sem)
     load.start()
 
@@ -166,13 +169,13 @@
     each(count - 1, push_p)
 
     line = lax.broadcasted_iota(jnp.int32, (8, rows), 0)
-    labels = jnp.where(line == 0, fold_row[...], jnp.where(line == 1, event_row[...], 0)).astype(F32)
+    labels = jnp.where(line == 0, code_row[...] // 2, jnp.where(line == 1, code_row[...] % 2, 0)).astype(F32)
     same = lax.broadcasted_iota(jnp.int32, (columns, columns), 0) == lax.broadcasted_iota(
         jnp.int32, (columns, columns), 1
     )
     pace = jnp.sum(jnp.where(same, step_row[...], 0.0), axis=1, keepdims=True)
     threshold = pace * jnp.sum(jnp.where(same, penalty_row[...], 0.0), axis=1, keepdims=True)
-    column_fold = lax.rem(lax.broadcasted_iota(jnp.int32, (columns, rows), 0), FOLDS).astype(F32)
+    column_fold = lax.rem(lax.broadcasted_iota(jnp.int32, (few, rows), 0) + var * few, FOLDS).astype(F32)
     mask[...] = jnp.where(labels[0:1, :] != column_fold, 1.0, 0.0)
     kept[...] = mask[...] * labels[1:2, :]
     ranks = lax.broadcasted_iota(jnp.int32, (rows, width), 0)
@@ -251,7 +254,7 @@
             relay_all(bit, fwd_ss, c_rs)
         each(half - 1, add_down)
         each(half, add_side)
-        half_send[...] = pred[...]
+        half_send[...] = pred[theirs, :]
         slot = lax.rem(turn, 2)
         swap = pltpu.make_async_remote_copy(
             src_ref=half_send, dst_ref=half_recv.at[slot], send_sem=half_ss, recv_sem=half_rs.at[slot],
@@ -264,8 +267,8 @@
         def _():
             settle(bit, c_ss, fwd_ss, c_rs)
 
-        weight = mask[...] * jnp.exp((half_send[...] + half_recv[slot]) * scale_vars)
-        pred[...] = weight
+        weight = mask[...] * jnp.exp((pred[mine, :] + half_recv[slot]) * scale_vars)
+        held[...] = weight
         spread = dot2(weight, to_time[...])
         for owner in range(count):
             out_a[owner] = spread[:, owner * width:(owner + 1) * width]
@@ -294,7 +297,13 @@
             owner = peer(step + 1)
             arrive(out_b.at[owner], in_b.at[owner], b_ss, b_rs, owner)
             hazard += across2(in_b[owner], to_id[:, slots(owner)])
-        score_out[...] = (pred[...] * hazard - kept[...]).astype(BF16)
+        score_out[mine, :] = (held[...] * hazard - kept[...]).astype(BF16)
+        trade = pltpu.make_async_remote_copy(
+            src_ref=score_out.at[mine, :], dst_ref=score_out.at[mine, :], send_sem=s_ss, recv_sem=s_rs,
+            device_id={"var": 1 - var}, device_id_type=MESH,
+        )
+        trade.start()
+        trade.wait()
 
         def push_g(step):
             owner = peer(step + 1)
@@ -375,7 +384,7 @@
             jax.ShapeDtypeStruct((columns, variants), F32),
             jax.ShapeDtypeStruct((columns, rows), BF16),
         ),
-        in_specs=[pl.BlockSpec(memory_space=pl.ANY)] + [vmem] * 9,
+        in_specs=[pl.BlockSpec(memory_space=pl.ANY)] + [vmem] * 8,
         out_specs=(vmem, vmem),
         scratch_shapes=[
             pltpu.VMEM((rows, variants), BF16),
@@ -383,23 +392,25 @@
             pltpu.VMEM((rows, total), BF16),
             pltpu.VMEM((rows, total), BF16),
             pltpu.VMEM((rows, total), BF16),
-            pltpu.VMEM((columns, rows), F32),
-            pltpu.VMEM((columns, rows), F32),
-            pltpu.VMEM((columns, rows), F32),
+            pltpu.VMEM((columns // 2, rows), F32),
+            pltpu.VMEM((columns // 2, rows), F32),
+            pltpu.VMEM((columns // 2, rows), F32),
             pltpu.VMEM((count, 1, width), jnp.int32),
             pltpu.VMEM((count, 8, width), F32),
             pltpu.VMEM((count, 8, width), F32),
             pltpu.VMEM((count, columns, part), BF16),
             pltpu.VMEM((columns, part), F32),
-            pltpu.VMEM((columns, rows), F32),
-            pltpu.VMEM((2, columns, rows), F32),
-            pltpu.VMEM((count, columns, width), F32),
-            pltpu.VMEM((count, columns, width), F32),
-            pltpu.VMEM((count, columns, width), F32),
-            pltpu.VMEM((count, columns, width), F32),
+            pltpu.VMEM((columns // 2, rows), F32),
+            pltpu.VMEM((2, columns // 2, rows), F32),
+            pltpu.VMEM((count, columns // 2, width), F32),
+            pltpu.VMEM((count, columns // 2, width), F32),
+            pltpu.VMEM((count, columns // 2, width), F32),
+            pltpu.VMEM((count, columns // 2, width), F32),
             pltpu.VMEM((count, columns, part), BF16),
             pltpu.VMEM((count, columns, part), BF16),
             pltpu.VMEM((columns, rows), F32),
+            pltpu.VMEM((columns // 2, rows), F32),
+            dma, dma,
             dma,
         ] + [dma((count,))] * 4 + [dma((count, CUTS))] * 2 + [
             dma, dma((2,)),
@@ -408,7 +419,7 @@
             collective_id=0, has_side_effects=True, vmem_limit_bytes=60 * 1024 * 1024
         ),
     )(
-        genotypes, coefficients, fold_label[None], event_flag[None], place_of, reach, back, spot,
+        genotypes, coefficients, (fold_label * 2 + event_flag)[None], place_of, reach, back, spot,
         step_size[None], penalty[None],
     )
 

time: 155 us -> 158 us (1.019)
  Pallas kernels: 143 us -> 147 us
  local copies, waits for them, and re-layouts: 6.21 us -> 4.26 us
    pallas_call x1, Pallas kernels: 143 us -> 147 us  [local(): pl.pallas_call(functools.partial(path_kernel, count, 1.0 / math.sqrt(VARS...]
    broadcast_in_dim x2 -> x1, local copies, waits for them, and re-layouts: 2.54 us -> 0.6 us  [local(): (fold_label * 2 + event_flag)[None]]
where the time goes in v4:
time: 158 us; the launch traced here: 157 us
  Pallas kernels  147 us (93%)
  other arithmetic  4.82 us (3%)
  local copies, waits for them, and re-layouts  4.26 us (3%)
    pallas_call x1, Pallas kernels, local(): pl.pallas_call(functools.partial(path_kernel, count, 1.0 / math.sqrt(VARS...  147 us
    unnamed x4, local copies, waits for them, and re-layouts  3.67 us

profile of v4, /device:TPU:24, one launch (start us, length us, event | category | flops | bytes accessed | tf_op | source)
XLA Modules:
  0.0 156.7 jit_solution(4934416921804673978)
XLA Ops:
  0.6 0.7 multiply_add_fusion.1
  1.3 0.6 broadcast_in_dim.44.code_row
  1.9 0.7 add_select_fusion.1
  2.6 0.2 convert_reduce_fusion
  2.9 0.7 add_select_fusion
  3.6 1.3 select_reduce_fusion
  4.9 0.6 compare_select_fusion.2
  5.5 0.0 copy-start
  5.5 0.6 and_select_fusion.reach
  6.1 0.0 copy-done
  6.1 146.9 %shard_map.86 = (f32[32,8192]{1,0:T(8,128)}, bf16[32,576]{1,0:T(8,128)(2,1)}) custom-call(bf16[576,8192]{1,0:T(8,128)(2,1)} %geno_in.1, f32[32,8192]{1,0:T(8,128)} %coef_in.1, s32[1,576]{1,0:T(1,128)} %broadcast_in_dim.44.code_row, s32[8,1,128]{2,1,0:T(1,128)} %bitcast.4, s32[8,1,128]{2,1,0:T(1,128)} %and_select_fusion.reach, ...), custom_call_target="tpu_custom_call" | custom-call | tf_op jit(solution)/shard_map/pallas_call | solution.py:381
  153.0 2.3 %copy.11 = f32[32,8192]{1,0:T(8,128)} copy(f32[32,8192]{1,0:T(8,128)} %get-tuple-element.10) | data formatting | bytes 2097152
  155.3 1.4 copy.12
Async XLA Ops:
  5.5 0.6 copy-start

commit v5 on v4

--- a/solution.py
+++ b/solution.py
@@ -12,7 +12,8 @@
 FOLDS = 8
 ITERS = 3
 MESH = pl.DeviceIdType.MESH
-CUTS = 8
+CUTS_LOW = 1
+CUTS = 4
 F32 = jnp.float32
 BF16 = jnp.bfloat16
 
@@ -80,14 +81,14 @@
     def down(step):
         return lax.rem(me + 2 * step, count)
 
-    cuts = min(CUTS, part // 128)
-    cut = part // cuts
+    cut = columns // CUTS
+    cut_low = columns // CUTS_LOW
 
     def bit(owner, number):
-        return low.at[owner, :, pl.ds(number * cut, cut)]
+        return low.at[owner, pl.ds(number * cut_low, cut_low), :]
 
     def wide(owner, number):
-        return coef_out.at[:, pl.ds(pl.multiple_of(owner * part + number * cut, cut), cut)]
+        return coef_out.at[pl.ds(number * cut, cut), piece(owner)]
 
     def send_to(spot_of, ssem, rsem, number, owner):
         return pltpu.make_async_remote_copy(
@@ -104,14 +105,14 @@
         )
 
     def spread_out(spot_of, ssem, rsem):
-        for number in range(cuts):
+        for number in range(CUTS_LOW if spot_of is bit else CUTS):
             def go(step):
                 send_to(spot_of, ssem, rsem, number, down(step + 1)).start()
             send_to(spot_of, ssem, rsem, number, me + side).start()
             each(half - 1, go)
 
     def relay_all(spot_of, ssem, rsem):
-        for number in range(cuts):
+        for number in range(CUTS_LOW if spot_of is bit else CUTS):
             def go(step):
                 copy = pass_on(spot_of, ssem, rsem, number, down(step + 1))
                 copy.wait_recv()
@@ -119,11 +120,11 @@
             each(half - 1, go)
 
     def land(spot_of, ssem, rsem, owner):
-        for number in range(cuts):
+        for number in range(CUTS_LOW if spot_of is bit else CUTS):
             pass_on(spot_of, ssem, rsem, number, owner).wait_recv()
 
     def settle(spot_of, ssem, fsem, rsem):
-        for number in range(cuts):
+        for number in range(CUTS_LOW if spot_of is bit else CUTS):
             def go(step):
                 owner = down(step + 1)
                 send_to(spot_of, ssem, rsem, number, owner).wait_send()

time: 158 us -> 153 us (0.968)
  Pallas kernels: 147 us -> 143 us
    pallas_call x1, Pallas kernels: 147 us -> 143 us  [local(): pl.pallas_call(functools.partial(path_kernel, count, 1.0 / math.sqrt(VARS...]
where the time goes in v5:
time: 153 us
  Pallas kernels  143 us (93%)
  other arithmetic  4.82 us (3%)
  local copies, waits for them, and re-layouts  4.26 us (3%)
    pallas_call x1, Pallas kernels, local(): pl.pallas_call(functools.partial(path_kernel, count, 1.0 / math.sqrt(VARS...  143 us
    unnamed x4, local copies, waits for them, and re-layouts  3.67 us

profile of v5, /device:TPU:24, one launch (start us, length us, event | category | flops | bytes accessed | tf_op | source)
XLA Modules:
  0.0 152.6 jit_solution(2113255937619801436)
XLA Ops:
  0.6 0.7 multiply_add_fusion.1
  1.3 0.6 broadcast_in_dim.44.code_row
  1.9 0.7 add_select_fusion.1
  2.6 0.2 convert_reduce_fusion
  2.9 0.7 add_select_fusion
  3.6 1.3 select_reduce_fusion
  4.9 0.6 compare_select_fusion.2
  5.5 0.0 copy-start
  5.5 0.6 and_select_fusion.reach
  6.1 0.0 copy-done
  6.1 142.9 %shard_map.86 = (f32[32,8192]{1,0:T(8,128)}, bf16[32,576]{1,0:T(8,128)(2,1)}) custom-call(bf16[576,8192]{1,0:T(8,128)(2,1)} %geno_in.1, f32[32,8192]{1,0:T(8,128)} %coef_in.1, s32[1,576]{1,0:T(1,128)} %broadcast_in_dim.44.code_row, s32[8,1,128]{2,1,0:T(1,128)} %bitcast.4, s32[8,1,128]{2,1,0:T(1,128)} %and_select_fusion.reach, ...), custom_call_target="tpu_custom_call" | custom-call | tf_op jit(solution)/shard_map/pallas_call | solution.py:382
  148.9 2.3 %copy.11 = f32[32,8192]{1,0:T(8,128)} copy(f32[32,8192]{1,0:T(8,128)} %get-tuple-element.10) | data formatting | bytes 2097152
  151.2 1.4 copy.12
Async XLA Ops:
  5.5 0.6 copy-start
